TPU v7x, 128 devices: a whole 4x4x4 slice. The times are simulated.
128 devices in a mesh: space: 64 (over x, y, z), sub: 2 (over core).
Axes of the slice: x: 4, y: 4, z: 4, core: 2. Of those that a mesh axis runs over, the one named last changes fastest.
Arguments:
- mode_rows: float32 [256, 1048576], P(None, ('space', 'sub')), as said below
- snapshots: float32 [3, 64, 1048576], P(None, None, ('space', 'sub')), as said below
- probe_fields: float32 [128, 1048576], P(None, ('space', 'sub')), as said below
- core_factor: float32 [256, 256], replicated, as said below
Outputs:
- new_modes: float32 [256, 1048576], P(None, ('space', 'sub'))
- new_core: float32 [256, 256], replicated
- captured: float32 [3, 256, 320], replicated
Inputs may be any that keep to these rules, and one draw needn't show every extreme that they name: `mode_rows`: rows of full rank, entries of order one. `snapshots`: fields of order one. `probe_fields`: fields of order one. `core_factor`: lower triangular with a positive diagonal.
All inputs are finite; a program needn't handle non-finite values.
Results may differ from a plain program's by a relative error of at most 0.0003.
Values sent between devices are 32-bit elements; how exact they have to be, the bound alone decides.
A program may use at most 128 MiB of HBM per device.

v0:
```python
import jax
import jax.numpy as jnp
from jax import lax
from jax.sharding import PartitionSpec as P

TURNS = 2
PRECISE = lax.Precision.HIGHEST


def row_inner(left, right):
    return lax.dot_general(left, right, (((1,), (1,)), ((), ())), precision=PRECISE)


def matmul_high(left, right):
    return jnp.dot(left, right, precision=PRECISE)


def block_cholesky(matrix):
    order = matrix.shape[0]
    width = 64
    lowered = jnp.zeros((order, order), jnp.float32)
    for start in range(0, order, width):
        finish = start + width
        done_rows = lowered[start:finish, :start]
        diag_block = matrix[start:finish, start:finish] - matmul_high(done_rows, done_rows.T)
        diag_factor = jnp.linalg.cholesky(diag_block)
        lowered = lowered.at[start:finish, start:finish].set(diag_factor)
        if finish < order:
            below = matrix[finish:, start:finish] - matmul_high(
                lowered[finish:, :start], done_rows.T
            )
            panel = jax.scipy.linalg.solve_triangular(diag_factor, below.T, lower=True).T
            lowered = lowered.at[finish:, start:finish].set(panel)
    return lowered


def update_core(core_now, projected, factor, turn_count):
    rank_count = core_now.shape[0]
    batch_count = factor.shape[0]
    upper = jnp.concatenate([core_now, projected], axis=1)
    bottom = jnp.concatenate([jnp.zeros((batch_count, rank_count), jnp.float32), factor.T], axis=1)
    stacked = jnp.concatenate([upper, bottom], axis=0)
    squared = matmul_high(stacked, stacked.T)
    rotation = jnp.eye(rank_count + batch_count, rank_count, dtype=jnp.float32)
    for sweep_index in range(turn_count):
        rotation = matmul_high(squared, rotation)
        lowered = block_cholesky(matmul_high(rotation.T, rotation))
        rotation = jax.scipy.linalg.solve_triangular(lowered, rotation.T, lower=True).T
    fresh_core = block_cholesky(matmul_high(rotation.T, matmul_high(squared, rotation)))
    return (rotation, fresh_core)


def orthonormalize(residual, volume):
    gram_local = row_inner(residual, residual)
    factor = block_cholesky(lax.psum(gram_local, ("space", "sub")) * volume)
    orthogonal = jax.scipy.linalg.solve_triangular(factor, residual, lower=True)
    return (factor, orthogonal)


def body(mode_rows, snapshots, probe_fields, core_factor):
    local_rows = mode_rows.shape[1]
    batch_count = snapshots.shape[0]
    batch_width = snapshots.shape[1]
    volume = 1.0 / (local_rows * lax.axis_size("space") * lax.axis_size("sub"))
    window = jnp.concatenate(
        [snapshots.reshape(batch_count * batch_width, local_rows), probe_fields], axis=0
    )
    basis_now = mode_rows
    core_now = core_factor
    captured = []
    for batch_index in range(batch_count):
        incoming = snapshots[batch_index]
        projected = lax.psum(row_inner(basis_now, incoming), ("space", "sub")) * volume
        residual = incoming - matmul_high(projected.T, basis_now)
        factor, orthogonal = orthonormalize(residual, volume)
        rotation, core_now = update_core(core_now, projected, factor, TURNS)
        basis_now = matmul_high(rotation.T, jnp.concatenate([basis_now, orthogonal], axis=0))
        captured.append(lax.psum(row_inner(basis_now, window), ("space", "sub")) * volume)
    return (basis_now, core_now, jnp.stack(captured))


def solution(mesh):
    return jax.shard_map(
        body,
        mesh=mesh,
        in_specs=(
            P(None, ("space", "sub")),
            P(None, None, ("space", "sub")),
            P(None, ("space", "sub")),
            P(),
        ),
        out_specs=(P(None, ("space", "sub")), P(), P()),
        check_vma=False,
    )
```

profile of v0, /device:TPU:1, one launch (start us, length us, event | category | flops | bytes accessed | tf_op | source)
XLA Modules:
  0.0 1623.2 jit_solution(15675498892306487198)
XLA Ops:
  7.2 10.0 fusion.19
  17.3 143.2 %all-reduce.18.cloned.1.call-done = f32[256,64]{1,0:T(8,128)} async-done(((f32[256,64]{1,0:T(8,128)}), f32[256,64]{1,0:T(8,128)}) %all-reduce.18.cloned.1.call-update) | async-done | bytes 65552 | tf_op jit(solution)/shard_map/psum | solution.py:73
  160.5 9.2 convolution_subtract_fusion.2
  171.5 63.6 %psum.64 = f32[64,64]{0,1:T(8,128)S(1)} all-reduce(f32[64,64]{0,1:T(8,128)S(1)} %fusion.442), channel_id=1, replica_groups=mesh['space'=64,'sub'=2] {'space','sub'}, use_global_device_ids=true, to_apply=%region_1.0 | all-reduce | flops 4096 | bytes 32768 | tf_op jit(solution)/shard_map/psum | solution.py:55
  235.2 5.8 cholesky.599
  245.5 5.8 cholesky.610
  258.9 5.8 cholesky.621
  308.2 20.1 %custom-call.51 = f32[2,128,128]{1,2,0:T(8,128)S(1)} custom-call(f32[2,128,128]{2,1,0:T(8,128)S(1)} %get-tuple-element.863), custom_call_target="InvertDiagBlocksLowerTriangular" | custom-call | tf_op jit(solution)/shard_map/jit(_solve_triangular)/triangular_solve | solution.py:48
  330.9 5.8 cholesky.654
  344.3 5.8 cholesky.665
  365.9 5.8 cholesky.676
  384.1 5.8 cholesky.687
  398.1 19.8 %custom-call.55 = f32[2,128,128]{1,2,0:T(8,128)S(1)} custom-call(f32[2,128,128]{2,1,0:T(8,128)S(1)} %get-tuple-element.864), custom_call_target="InvertDiagBlocksLowerTriangular" | custom-call | tf_op jit(solution)/shard_map/jit(_solve_triangular)/triangular_solve | solution.py:48
  420.5 5.8 cholesky.698
  433.3 5.8 cholesky.709
  459.8 5.8 cholesky.720
  480.7 16.3 %fusion = f32[256,8192]{1,0:T(8,128)S(1)} fusion(f32[64,8192]{1,0:T(8,128)} %fusion.189, f32[256,8192]{1,0:T(8,128)} %param.153, f32[128,320]{0,1:T(8,128)S(1)} %fusion.125, f32[128,320]{0,1:T(8,128)S(1)} %fusion.98), kind=kOutput, calls=%fused_computation.12 | convolution fusion | flops 8055767040 | bytes 19202048 | tf_op jit(solution)/shard_map/dot_general | solution.py:15
  500.4 8.9 fusion.17
  509.3 13.3 fusion.14
  524.3 122.0 %all-reduce.20.cloned.1.call-done = f32[256,64]{1,0:T(8,128)} async-done(((f32[256,64]{1,0:T(8,128)}), f32[256,64]{1,0:T(8,128)}) %all-reduce.20.cloned.1.call-update) | async-done | bytes 65552 | tf_op jit(solution)/shard_map/psum | solution.py:73
  646.3 9.2 convolution_subtract_fusion.1
  657.2 63.7 %psum.66 = f32[64,64]{0,1:T(8,128)S(1)} all-reduce(f32[64,64]{0,1:T(8,128)S(1)} %fusion.445), channel_id=1, replica_groups=mesh['space'=64,'sub'=2] {'space','sub'}, use_global_device_ids=true, to_apply=%region_5.12 | all-reduce | flops 4096 | bytes 32768 | tf_op jit(solution)/shard_map/psum | solution.py:55
  721.0 5.8 cholesky.742
  731.3 5.8 cholesky.753
  744.8 5.8 cholesky.764
  766.3 5.8 cholesky.775
  782.2 5.8 cholesky.786
  794.5 19.8 %custom-call.63 = f32[2,128,128]{1,2,0:T(8,128)S(1)} custom-call(f32[2,128,128]{2,1,0:T(8,128)S(1)} %get-tuple-element.865), custom_call_target="InvertDiagBlocksLowerTriangular" | custom-call | tf_op jit(solution)/shard_map/jit(_solve_triangular)/triangular_solve | solution.py:48
  816.9 5.8 cholesky.797
  830.4 5.8 cholesky.808
  852.1 5.8 cholesky.819
  870.4 5.8 cholesky.830
  884.3 19.9 %custom-call.67 = f32[2,128,128]{1,2,0:T(8,128)S(1)} custom-call(f32[2,128,128]{2,1,0:T(8,128)S(1)} %get-tuple-element.866), custom_call_target="InvertDiagBlocksLowerTriangular" | custom-call | tf_op jit(solution)/shard_map/jit(_solve_triangular)/triangular_solve | solution.py:48
  906.7 5.8 cholesky.841
  944.9 17.2 %fusion.4 = f32[256,8192]{1,0:T(8,128)S(1)} fusion(f32[64,8192]{1,0:T(8,128)S(1)} %fusion.165, f32[256,8192]{1,0:T(8,128)} %copy-done.1, f32[128,320]{0,1:T(8,128)S(1)} %fusion.115, f32[128,320]{0,1:T(8,128)S(1)} %fusion.94), kind=kOutput, calls=%fused_computation.16 | convolution fusion | flops 8055767040 | bytes 19202048 | tf_op jit(solution)/shard_map/dot_general | solution.py:15
  965.3 8.9 fusion.15
  974.2 13.1 fusion.13
  1010.1 114.5 %all-reduce.22.cloned.1.call-done = f32[256,64]{1,0:T(8,128)} async-done(((f32[256,64]{1,0:T(8,128)}), f32[256,64]{1,0:T(8,128)}) %all-reduce.22.cloned.1.call-update) | async-done | bytes 65552 | tf_op jit(solution)/shard_map/psum | solution.py:73
  1124.6 9.2 convolution_subtract_fusion
  1135.6 63.8 %psum.68 = f32[64,64]{0,1:T(8,128)S(1)} all-reduce(f32[64,64]{0,1:T(8,128)S(1)} %fusion.448), channel_id=1, replica_groups=mesh['space'=64,'sub'=2] {'space','sub'}, use_global_device_ids=true, to_apply=%region_7.14 | all-reduce | flops 4096 | bytes 32768 | tf_op jit(solution)/shard_map/psum | solution.py:55
  1209.8 5.8 cholesky.896
  1272.4 19.9 %custom-call.75 = f32[2,128,128]{1,2,0:T(8,128)S(1)} custom-call(f32[2,128,128]{2,1,0:T(8,128)S(1)} %get-tuple-element.867), custom_call_target="InvertDiagBlocksLowerTriangular" | custom-call | tf_op jit(solution)/shard_map/jit(_solve_triangular)/triangular_solve | solution.py:48
  1294.9 5.8 cholesky.940
  1362.3 20.1 %custom-call.79 = f32[2,128,128]{1,2,0:T(8,128)S(1)} custom-call(f32[2,128,128]{2,1,0:T(8,128)S(1)} %get-tuple-element.868), custom_call_target="InvertDiagBlocksLowerTriangular" | custom-call | tf_op jit(solution)/shard_map/jit(_solve_triangular)/triangular_solve | solution.py:48
  1384.9 5.8 cholesky.984
  1422.8 18.3 %fusion.8 = f32[256,8192]{1,0:T(8,128)} fusion(f32[64,8192]{1,0:T(8,128)S(1)} %fusion.148, f32[256,8192]{1,0:T(8,128)} %copy-done, f32[128,320]{0,1:T(8,128)S(1)} %fusion.105, f32[128,320]{0,1:T(8,128)S(1)} %fusion.90), kind=kOutput, calls=%fused_computation.20 | convolution fusion | flops 8055767040 | bytes 19202048 | tf_op jit(solution)/shard_map/dot_general | solution.py:15
  1455.7 13.1 fusion.12
  1477.1 136.2 %all-reduce.24.cloned.1.call-done = (f32[256,320]{0,1:T(8,128)}, f32[256,320]{0,1:T(8,128)}, f32[256,320]{0,1:T(8,128)}) async-done(((f32[256,320]{0,1:T(8,128)}, f32[256,320]{0,1:T(8,128)}, f32[256,320]{0,1:T(8,128)}), (f32[256,320]{0,1:T(8,128)}, f32[256,320]{0,1:T(8,128)}, f32[256,320]{0,1:T(8,128)})) %all-reduce.24.cloned.1.call-update) | async-done | bytes 983056 | tf_op jit(solution)/shard_map/psum | solution.py:78
  (535 shorter events, 522.5 us)
Async XLA Ops:
  7.2 153.3 %all-reduce.18.cloned.1.call-start = ((), (), s32[]{:S(2)}) async-start(), calls=%async_computation | async-start | bytes 262144 | tf_op jit(solution)/shard_map/psum | solution.py:73
  17.2 629.1 %all-reduce.20.cloned.1.call-start = ((), (), s32[]{:S(2)}) async-start(), calls=%async_computation.1 | async-start | bytes 262144 | tf_op jit(solution)/shard_map/psum | solution.py:73
  17.3 225.8 %copy-start.9 = (f32[256,256]{1,0:T(8,128)S(1)}, f32[256,256]{1,0:T(8,128)}, u32[]{:S(2)}) copy-start(f32[256,256]{1,0:T(8,128)} %param.156) | copy-start | bytes 786436
  160.5 82.5 %copy-start.6 = (f32[256,64]{1,0:T(8,128)S(1)}, f32[256,64]{1,0:T(8,128)}, u32[]{:S(2)}) copy-start(f32[256,64]{1,0:T(8,128)} %all-reduce.18.cloned.1.call-done) | copy-start | bytes 196612
  245.4 34.5 %copy-start.2 = (f32[256,256]{0,1:T(8,128)}, f32[256,256]{0,1:T(8,128)S(1)}, u32[]{:S(2)}) copy-start(f32[256,256]{0,1:T(8,128)S(1)} %fusion.443) | copy-start | bytes 786436
  497.0 3.4 copy-start.1
  509.3 615.3 %all-reduce.22.cloned.1.call-start = ((), (), s32[]{:S(2)}) async-start(), calls=%async_computation.2 | async-start | bytes 262144 | tf_op jit(solution)/shard_map/psum | solution.py:73
  646.3 82.6 %copy-start.7 = (f32[256,64]{1,0:T(8,128)S(1)}, f32[256,64]{1,0:T(8,128)}, u32[]{:S(2)}) copy-start(f32[256,64]{1,0:T(8,128)} %all-reduce.20.cloned.1.call-done) | copy-start | bytes 196612
  731.2 34.8 %copy-start.3 = (f32[256,256]{0,1:T(8,128)}, f32[256,256]{0,1:T(8,128)S(1)}, u32[]{:S(2)}) copy-start(f32[256,256]{0,1:T(8,128)S(1)} %fusion.446) | copy-start | bytes 786436
  962.1 3.2 copy-start
  987.3 626.0 %all-reduce.24.cloned.1.call-start = ((), (), s32[]{:S(2)}) async-start(), calls=%async_computation.3 | async-start | bytes 1966080 | tf_op jit(solution)/shard_map/psum | solution.py:78
  1124.6 82.8 %copy-start.5 = (f32[256,64]{1,0:T(8,128)S(1)}, f32[256,64]{1,0:T(8,128)}, u32[]{:S(2)}) copy-start(f32[256,64]{1,0:T(8,128)} %all-reduce.22.cloned.1.call-done) | copy-start | bytes 196612
  1209.7 34.4 %copy-start.4 = (f32[256,256]{0,1:T(8,128)}, f32[256,256]{0,1:T(8,128)S(1)}, u32[]{:S(2)}) copy-start(f32[256,256]{0,1:T(8,128)S(1)} %fusion.449) | copy-start | bytes 786436
  1477.0 139.4 %copy-start.8 = (f32[256,256]{1,0:T(8,128)}, f32[256,256]{1,0:T(8,128)S(1)}, u32[]{:S(2)}) copy-start(f32[256,256]{1,0:T(8,128)S(1)} %scatter.314) | copy-start | bytes 786436
Sparse Core Ops, SparseCore 0:
  17.3 143.1 all-reduce.17
  509.4 136.8 all-reduce.19
  987.5 137.0 all-reduce.21
  1469.0 144.2 all-reduce.23
where the time goes:
time: 1630 us; the launch traced here: 1620 us
  other arithmetic  568 us (35%)
  waiting for transfers between devices  516 us (32%)
  matrix products  212 us (13%)
  blocking collectives  191 us (12%)
  local copies, waits for them, and re-layouts  118 us (7%)
  between operations  16.6 us (1%)
    psum x3, waiting for transfers between devices, body(): lax.psum(row_inner(basis_now, incoming), ('space', 'sub')) * volume  380 us
    another operation x117, other arithmetic, block_cholesky(): diag_factor = jnp.linalg.cholesky(diag_block)  255 us
    psum x3, blocking collectives, orthonormalize(): factor = block_cholesky(lax.psum(gram_local, ('space', 'sub')) * volume)  191 us
    another operation x54, other arithmetic, block_cholesky(): jax.scipy.linalg.solve_triangular(diag_factor, below.T, lower=True)  161 us
    psum x1, waiting for transfers between devices, body(): lax.psum(row_inner(basis_now, window), ('space', 'sub')) * volume  136 us
    another operation x13, other arithmetic, update_core(): jax.scipy.linalg.solve_triangular(lowered, rotation.T, lower=True)  123 us
    dot_general x72, matrix products, matmul_high(): return jnp.dot(left, right, precision=PRECISE)  114 us
    dot_general x9, matrix products, row_inner(): lax.dot_general(left, right, (((1,), (1,)), ((), ())), precision=PRECISE)  72.7 us
  transfers between devices with their start and end apart: 4, of which 4 were waited for; matrix products, arithmetic and copies ran while one was open for 3% of the time, Pallas kernels for 0%

commit v1 on v0

--- a/solution.py
+++ b/solution.py
@@ -70,7 +70,10 @@
     captured = []
     for batch_index in range(batch_count):
         incoming = snapshots[batch_index]
-        projected = lax.psum(row_inner(basis_now, incoming), ("space", "sub")) * volume
+        projected = (
+            jnp.sum(lax.all_gather(row_inner(basis_now, incoming), ("space", "sub")), axis=0)
+            * volume
+        )
         residual = incoming - matmul_high(projected.T, basis_now)
         factor, orthogonal = orthonormalize(residual, volume)
         rotation, core_now = update_core(core_now, projected, factor, TURNS)

time: 1630 us -> 1370 us (0.84)
  waiting for transfers between devices: 516 us -> 232 us
    psum x3 -> x0, waiting for transfers between devices: 380 us -> none  [body(): lax.psum(row_inner(basis_now, incoming), ('space', 'sub')) * volume]
    all_gather x0 -> x3, waiting for transfers between devices: none -> 96 us  [body(): lax.all_gather(row_inner(basis_now, incoming), ('space', 'sub'))]
  transfers between devices with their start and end apart: 4 -> 4, of which waited for: 4 -> 3; matrix products, arithmetic and copies ran while one was open for 3% -> 11% of each run, Pallas kernels for 0% -> 0%
where the time goes in v1:
time: 1370 us; the launch traced here: 1360 us
  other arithmetic  571 us (42%)
  waiting for transfers between devices  232 us (17%)
  matrix products  216 us (16%)
  blocking collectives  194 us (14%)
  local copies, waits for them, and re-layouts  129 us (9%)
  between operations  16.7 us (1%)
    another operation x117, other arithmetic, block_cholesky(): diag_factor = jnp.linalg.cholesky(diag_block)  255 us
    psum x3, blocking collectives, orthonormalize(): factor = block_cholesky(lax.psum(gram_local, ('space', 'sub')) * volume)  194 us
    another operation x54, other arithmetic, block_cholesky(): jax.scipy.linalg.solve_triangular(diag_factor, below.T, lower=True)  161 us
    psum x1, waiting for transfers between devices, body(): lax.psum(row_inner(basis_now, window), ('space', 'sub')) * volume  136 us
    another operation x13, other arithmetic, update_core(): jax.scipy.linalg.solve_triangular(lowered, rotation.T, lower=True)  121 us
    dot_general x72, matrix products, matmul_high(): return jnp.dot(left, right, precision=PRECISE)  112 us
    all_gather x3, waiting for transfers between devices, body(): lax.all_gather(row_inner(basis_now, incoming), ('space', 'sub'))  96 us
    dot_general x9, matrix products, row_inner(): lax.dot_general(left, right, (((1,), (1,)), ((), ())), precision=PRECISE)  77.5 us
  transfers between devices with their start and end apart: 4, of which 3 were waited for; matrix products, arithmetic and copies ran while one was open for 11% of the time, Pallas kernels for 0%

profile of v1, /device:TPU:1, one launch (start us, length us, event | category | flops | bytes accessed | tf_op | source)
XLA Modules:
  0.0 1359.5 jit_solution(2844324064561321461)
XLA Ops:
  7.2 12.3 fusion.19
  19.8 77.9 %all-gather.7.cloned.1.call-done = f32[32768,64]{0,1:T(8,128)} async-done(((f32[256,64]{0,1:T(8,128)}), f32[32768,64]{0,1:T(8,128)}) %all-gather.7.cloned.1.call-update) | async-done | bytes 8388624 | tf_op jit(solution)/shard_map/all_gather | solution.py:74
  97.7 5.9 copy.247
  105.2 9.1 convolution_subtract_fusion.2
  116.1 64.6 %psum.42 = f32[64,64]{0,1:T(8,128)S(1)} all-reduce(f32[64,64]{0,1:T(8,128)S(1)} %fusion.442), channel_id=1, replica_groups=mesh['space'=64,'sub'=2] {'space','sub'}, use_global_device_ids=true, to_apply=%region_1.0 | all-reduce | flops 4096 | bytes 32768 | tf_op jit(solution)/shard_map/psum | solution.py:55
  180.8 5.8 cholesky.599
  191.1 5.8 cholesky.610
  204.6 5.8 cholesky.621
  225.9 5.8 cholesky.632
  241.8 5.8 cholesky.643
  254.0 20.1 %custom-call.51 = f32[2,128,128]{1,2,0:T(8,128)S(1)} custom-call(f32[2,128,128]{2,1,0:T(8,128)S(1)} %get-tuple-element.863), custom_call_target="InvertDiagBlocksLowerTriangular" | custom-call | tf_op jit(solution)/shard_map/jit(_solve_triangular)/triangular_solve | solution.py:48
  276.7 5.8 cholesky.654
  290.3 5.8 cholesky.665
  320.4 5.8 cholesky.676
  336.2 5.8 cholesky.687
  348.4 19.7 %custom-call.55 = f32[2,128,128]{1,2,0:T(8,128)S(1)} custom-call(f32[2,128,128]{2,1,0:T(8,128)S(1)} %get-tuple-element.864), custom_call_target="InvertDiagBlocksLowerTriangular" | custom-call | tf_op jit(solution)/shard_map/jit(_solve_triangular)/triangular_solve | solution.py:48
  369.0 16.1 %fusion = f32[256,8192]{1,0:T(8,128)S(1)} fusion(f32[64,8192]{1,0:T(8,128)} %fusion.189, f32[256,8192]{1,0:T(8,128)} %param.153, f32[128,320]{0,1:T(8,128)S(1)} %fusion.125, f32[128,320]{0,1:T(8,128)S(1)} %fusion.98), kind=kOutput, calls=%fused_computation.12 | convolution fusion | flops 8055767040 | bytes 19202048 | tf_op jit(solution)/shard_map/dot_general | solution.py:15
  388.5 10.0 fusion.17
  400.2 5.8 cholesky.698
  413.0 5.9 cholesky.709
  430.8 5.8 cholesky.720
  445.1 5.8 cholesky.731
  453.3 18.1 %all-gather.9.cloned.1.call-done = f32[32768,64]{0,1:T(8,128)} async-done(((f32[256,64]{0,1:T(8,128)}), f32[32768,64]{0,1:T(8,128)}) %all-gather.9.cloned.1.call-update) | async-done | bytes 8388624 | tf_op jit(solution)/shard_map/all_gather | solution.py:74
  471.4 5.9 copy.248
  479.1 9.1 convolution_subtract_fusion.1
  490.0 64.5 %psum.43 = f32[64,64]{0,1:T(8,128)S(1)} all-reduce(f32[64,64]{0,1:T(8,128)S(1)} %fusion.445), channel_id=1, replica_groups=mesh['space'=64,'sub'=2] {'space','sub'}, use_global_device_ids=true, to_apply=%region_5.12 | all-reduce | flops 4096 | bytes 32768 | tf_op jit(solution)/shard_map/psum | solution.py:55
  554.5 5.8 cholesky.742
  564.8 5.8 cholesky.753
  578.2 5.8 cholesky.764
  627.8 20.1 %custom-call.63 = f32[2,128,128]{1,2,0:T(8,128)S(1)} custom-call(f32[2,128,128]{2,1,0:T(8,128)S(1)} %get-tuple-element.865), custom_call_target="InvertDiagBlocksLowerTriangular" | custom-call | tf_op jit(solution)/shard_map/jit(_solve_triangular)/triangular_solve | solution.py:48
  650.5 5.8 cholesky.797
  722.0 19.7 %custom-call.67 = f32[2,128,128]{1,2,0:T(8,128)S(1)} custom-call(f32[2,128,128]{2,1,0:T(8,128)S(1)} %get-tuple-element.866), custom_call_target="InvertDiagBlocksLowerTriangular" | custom-call | tf_op jit(solution)/shard_map/jit(_solve_triangular)/triangular_solve | solution.py:48
  742.6 16.1 %fusion.4 = f32[256,8192]{1,0:T(8,128)S(1)} fusion(f32[64,8192]{1,0:T(8,128)} %fusion.165, f32[256,8192]{1,0:T(8,128)} %copy-done.1, f32[128,320]{0,1:T(8,128)S(1)} %fusion.115, f32[128,320]{0,1:T(8,128)S(1)} %fusion.94), kind=kOutput, calls=%fused_computation.16 | convolution fusion | flops 8055767040 | bytes 19202048 | tf_op jit(solution)/shard_map/dot_general | solution.py:15
  762.0 10.0 fusion.15
  772.0 13.5 fusion.14
  787.2 5.8 cholesky.841
  840.0 13.3 fusion.13
  853.3 5.9 copy.249
  861.0 9.1 convolution_subtract_fusion
  871.9 64.5 %psum.44 = f32[64,64]{0,1:T(8,128)S(1)} all-reduce(f32[64,64]{0,1:T(8,128)S(1)} %fusion.448), channel_id=1, replica_groups=mesh['space'=64,'sub'=2] {'space','sub'}, use_global_device_ids=true, to_apply=%region_7.14 | all-reduce | flops 4096 | bytes 32768 | tf_op jit(solution)/shard_map/psum | solution.py:55
  946.9 5.8 cholesky.896
  1009.4 19.9 %custom-call.75 = f32[2,128,128]{1,2,0:T(8,128)S(1)} custom-call(f32[2,128,128]{2,1,0:T(8,128)S(1)} %get-tuple-element.867), custom_call_target="InvertDiagBlocksLowerTriangular" | custom-call | tf_op jit(solution)/shard_map/jit(_solve_triangular)/triangular_solve | solution.py:48
  1031.8 5.8 cholesky.940
  1099.0 20.1 %custom-call.79 = f32[2,128,128]{1,2,0:T(8,128)S(1)} custom-call(f32[2,128,128]{2,1,0:T(8,128)S(1)} %get-tuple-element.868), custom_call_target="InvertDiagBlocksLowerTriangular" | custom-call | tf_op jit(solution)/shard_map/jit(_solve_triangular)/triangular_solve | solution.py:48
  1121.6 5.8 cholesky.984
  1159.5 18.3 %fusion.8 = f32[256,8192]{1,0:T(8,128)} fusion(f32[64,8192]{1,0:T(8,128)S(1)} %fusion.148, f32[256,8192]{1,0:T(8,128)} %copy-done, f32[128,320]{0,1:T(8,128)S(1)} %fusion.105, f32[128,320]{0,1:T(8,128)S(1)} %fusion.90), kind=kOutput, calls=%fused_computation.20 | convolution fusion | flops 8055767040 | bytes 19202048 | tf_op jit(solution)/shard_map/dot_general | solution.py:15
  1192.4 13.1 fusion.12
  1213.8 135.9 %all-reduce.15.cloned.1.call-done = (f32[256,320]{0,1:T(8,128)}, f32[256,320]{0,1:T(8,128)}, f32[256,320]{0,1:T(8,128)}) async-done(((f32[256,320]{0,1:T(8,128)}, f32[256,320]{0,1:T(8,128)}, f32[256,320]{0,1:T(8,128)}), (f32[256,320]{0,1:T(8,128)}, f32[256,320]{0,1:T(8,128)}, f32[256,320]{0,1:T(8,128)})) %all-reduce.15.cloned.1.call-update) | async-done | bytes 983056 | tf_op jit(solution)/shard_map/psum | solution.py:81
  (542 shorter events, 531.0 us)
Async XLA Ops:
  7.2 90.5 %all-gather.7.cloned.1.call-start = ((), (), s32[]{:S(2)}) async-start(), calls=%async_computation | async-start | bytes 8454144 | tf_op jit(solution)/shard_map/all_gather | solution.py:74
  19.6 451.8 %all-gather.9.cloned.1.call-start = ((), (), s32[]{:S(2)}) async-start(), calls=%async_computation.1 | async-start | bytes 8454144 | tf_op jit(solution)/shard_map/all_gather | solution.py:74
  105.2 83.5 %copy-start.8 = (f32[256,256]{1,0:T(8,128)S(1)}, f32[256,256]{1,0:T(8,128)}, u32[]{:S(2)}) copy-start(f32[256,256]{1,0:T(8,128)} %param.156) | copy-start | bytes 786436
  191.0 34.6 %copy-start.4 = (f32[256,256]{0,1:T(8,128)}, f32[256,256]{0,1:T(8,128)S(1)}, u32[]{:S(2)}) copy-start(f32[256,256]{0,1:T(8,128)S(1)} %fusion.443) | copy-start | bytes 786436
  276.6 34.6 %copy-start.2 = (f32[256,256]{0,1:T(8,128)}, f32[256,256]{0,1:T(8,128)S(1)}, u32[]{:S(2)}) copy-start(f32[256,256]{0,1:T(8,128)S(1)} %fusion.444) | copy-start | bytes 786436
  385.1 3.4 copy-start.1
  398.5 454.8 %all-gather.11.cloned.1.call-start = ((), (), s32[]{:S(2)}) async-start(), calls=%async_computation.2 | async-start | bytes 8454144 | tf_op jit(solution)/shard_map/all_gather | solution.py:74
  564.7 34.5 %copy-start.5 = (f32[256,256]{0,1:T(8,128)}, f32[256,256]{0,1:T(8,128)S(1)}, u32[]{:S(2)}) copy-start(f32[256,256]{0,1:T(8,128)S(1)} %fusion.446) | copy-start | bytes 786436
  650.4 34.4 %copy-start.3 = (f32[256,256]{0,1:T(8,128)}, f32[256,256]{0,1:T(8,128)S(1)}, u32[]{:S(2)}) copy-start(f32[256,256]{0,1:T(8,128)S(1)} %fusion.447) | copy-start | bytes 786436
  758.7 3.2 copy-start
  771.9 577.7 %all-reduce.15.cloned.1.call-start = ((), (), s32[]{:S(2)}) async-start(), calls=%async_computation.3 | async-start | bytes 1966080 | tf_op jit(solution)/shard_map/psum | solution.py:81
  946.7 34.3 %copy-start.6 = (f32[256,256]{0,1:T(8,128)}, f32[256,256]{0,1:T(8,128)S(1)}, u32[]{:S(2)}) copy-start(f32[256,256]{0,1:T(8,128)S(1)} %fusion.449) | copy-start | bytes 786436
  1213.7 139.0 %copy-start.7 = (f32[256,256]{1,0:T(8,128)}, f32[256,256]{1,0:T(8,128)S(1)}, u32[]{:S(2)}) copy-start(f32[256,256]{1,0:T(8,128)S(1)} %scatter.314) | copy-start | bytes 786436
Sparse Core Ops, SparseCore 0:
  19.7 77.9 all-gather.6
  398.6 72.7 all-gather.8
  772.1 72.4 all-gather.10
  1205.7 143.8 all-reduce.14
